TPU v7x, 256 devices: a whole 4x4x8 slice. The times are simulated.
256 devices in a mesh: gx: 16 (over z_lo, x), gy: 2 (over core), gz: 8 (over z_hi, y).
Axes of the slice: x: 4, y: 4, z: 8 (z_hi: 2, z_lo: 4; z = z_hi * 4 + z_lo), core: 2. Of those that a mesh axis runs over, the one named last changes fastest.
Arguments:
- tokens: bfloat16 [128, 32, 128, 192], P('gx', 'gy', 'gz'), may hold values from -6 to 6
- upstream: bfloat16 [128, 32, 128, 192], P('gx', 'gy', 'gz'), may hold values from -6 to 6
- norm_gain: float32 [192], replicated, may hold values from 0.25 to 1.75
- norm_bias: float32 [192], replicated, may hold values from -3 to 3
- qkv_weight: bfloat16 [192, 576], replicated, may hold values from -4 to 4, as said below
- qkv_bias: float32 [576], replicated, may hold values from -3 to 3
- proj_weight: bfloat16 [192, 192], replicated, may hold values from -0.4375 to 0.4375
Outputs:
- token_grad: bfloat16 [128, 32, 128, 192], P('gx', 'gy', 'gz')
- qkv_weight_grad: float32 [192, 576], replicated
- qkv_bias_grad: float32 [576], replicated
- proj_weight_grad: float32 [192, 192], replicated
- proj_bias_grad: float32 [192], replicated
- gain_grad: float32 [192], replicated
- norm_bias_grad: float32 [192], replicated
Inputs may be any that keep to these rules, and one draw needn't show every extreme that they name: `qkv_weight`: columns are the query, key and value projections in that order, each 6 heads of 32 columns.
All inputs are finite; a program needn't handle non-finite values.
Results may differ from a plain program's by a relative error of at most 0.02.
The roundings to bfloat16 on the way count: a program that leaves them out, or rounds other values in their place, can miss the bound.
Values may be sent and summed in bfloat16 or wider, within the bound.
No kernel may reach another device: no remote copies, remote signals or barrier semaphores. Data moves between devices by JAX's collectives and lax.ppermute only.
A program may use at most 64 MiB of HBM per device.

v0:
```python
import jax
import jax.numpy as jnp
from jax import lax
from jax.sharding import PartitionSpec as P

HEADS = 6
WIN = 8
SHIFT = 4


def passed_along(value, axis, steps):
    count = lax.axis_size(axis)
    pairs = [(source, (source + steps) % count) for source in range(count)]
    return lax.ppermute(value, axis, pairs)


def window_grads(tok, upward, idents, norm_gain, norm_bias, qkv_weight, qkv_bias, proj_weight):
    length = tok.shape[0]
    width = tok.shape[1]
    heads = HEADS
    head_size = width // heads
    single = jnp.float32
    factor = head_size ** (-0.5)
    inputs = tok.astype(single)
    centred = inputs - jnp.mean(inputs, axis=-1, keepdims=True)
    inverse = lax.rsqrt(jnp.mean(centred * centred, axis=-1, keepdims=True) + 1e-05)
    normed = centred * inverse
    hidden = (normed * norm_gain + norm_bias).astype(jnp.bfloat16)
    packed = (jnp.dot(hidden, qkv_weight, preferred_element_type=single) + qkv_bias).astype(
        jnp.bfloat16
    )
    query = packed[:, :width].reshape(length, heads, head_size)
    keyset = packed[:, width : 2 * width].reshape(length, heads, head_size)
    valset = packed[:, 2 * width :].reshape(length, heads, head_size)
    scores = jnp.einsum("qhd,khd->hqk", query, keyset, preferred_element_type=single) * factor
    same = idents[:, None] == idents[None, :]
    scores = jnp.where(same[None], scores, -1e30)
    peak = jnp.max(scores, axis=-1, keepdims=True)
    expo = jnp.exp(scores - peak)
    probs = expo / jnp.sum(expo, axis=-1, keepdims=True)
    probs_half = probs.astype(jnp.bfloat16)
    attended = jnp.einsum("hqk,khd->qhd", probs_half, valset, preferred_element_type=single)
    attended = attended.reshape(length, width).astype(jnp.bfloat16)
    grad_proj = jnp.einsum("lc,lf->cf", attended, upward, preferred_element_type=single)
    grad_pbias = jnp.sum(upward.astype(single), axis=0)
    attended_grad = jnp.einsum(
        "lf,cf->lc", upward, proj_weight, preferred_element_type=single
    ).astype(jnp.bfloat16)
    attended_grad = attended_grad.reshape(length, heads, head_size)
    prob_grad = jnp.einsum("qhd,khd->hqk", attended_grad, valset, preferred_element_type=single)
    inner = jnp.sum(probs * prob_grad, axis=-1, keepdims=True)
    score_grad = (probs * (prob_grad - inner) * factor).astype(jnp.bfloat16)
    query_grad = jnp.einsum(
        "hqk,khd->qhd", score_grad, keyset, preferred_element_type=single
    ).reshape(length, width)
    key_grad = jnp.einsum("hqk,qhd->khd", score_grad, query, preferred_element_type=single).reshape(
        length, width
    )
    value_grad = jnp.einsum(
        "hqk,qhd->khd", probs_half, attended_grad, preferred_element_type=single
    ).reshape(length, width)
    packed_grad = jnp.concatenate([query_grad, key_grad, value_grad], axis=1).astype(jnp.bfloat16)
    grad_qkv = jnp.einsum("lc,lf->cf", hidden, packed_grad, preferred_element_type=single)
    grad_qbias = jnp.sum(packed_grad.astype(single), axis=0)
    hidden_grad = jnp.einsum("lf,cf->lc", packed_grad, qkv_weight, preferred_element_type=single)
    grad_gain = jnp.sum(hidden_grad * normed, axis=0)
    grad_nbias = jnp.sum(hidden_grad, axis=0)
    normed_grad = hidden_grad * norm_gain
    first = jnp.mean(normed_grad, axis=-1, keepdims=True)
    second = jnp.mean(normed_grad * normed, axis=-1, keepdims=True)
    token_grad = (upward.astype(single) + inverse * (normed_grad - first - normed * second)).astype(
        jnp.bfloat16
    )
    return (token_grad, (grad_qkv, grad_qbias, grad_proj, grad_pbias, grad_gain, grad_nbias))


def to_windows(block):
    sizes = block.shape[:3]
    rest = block.shape[3:]
    shaped = block.reshape(
        (sizes[0] // WIN, WIN, sizes[1] // WIN, WIN, sizes[2] // WIN, WIN) + rest
    )
    order = (0, 2, 4, 1, 3, 5) + tuple(range(6, 6 + len(rest)))
    return shaped.transpose(order).reshape((-1, WIN**3) + rest)


def from_windows(wins, first, second, third):
    rest = wins.shape[2:]
    shaped = wins.reshape((first // WIN, second // WIN, third // WIN, WIN, WIN, WIN) + rest)
    order = (0, 3, 1, 4, 2, 5) + tuple(range(6, 6 + len(rest)))
    return shaped.transpose(order).reshape((first, second, third) + rest)


def move_first(pieces):
    sent = passed_along((pieces[0][:SHIFT], pieces[1][:SHIFT]), "gx", -1)
    return (
        jnp.concatenate([pieces[0][SHIFT:], sent[0]], axis=0),
        jnp.concatenate([pieces[1][SHIFT:], sent[1]], axis=0),
    )


def move_second(pieces):
    sent = passed_along((pieces[0][:, :SHIFT], pieces[1][:, :SHIFT]), "gy", -1)
    return (
        jnp.concatenate([pieces[0][:, SHIFT:], sent[0]], axis=1),
        jnp.concatenate([pieces[1][:, SHIFT:], sent[1]], axis=1),
    )


def move_third(pieces):
    sent = passed_along((pieces[0][:, :, :SHIFT], pieces[1][:, :, :SHIFT]), "gz", -1)
    return (
        jnp.concatenate([pieces[0][:, :, SHIFT:], sent[0]], axis=2),
        jnp.concatenate([pieces[1][:, :, SHIFT:], sent[1]], axis=2),
    )


def window_index(count, position, length):
    total = length * count
    rolled = position * length + jnp.arange(length, dtype=jnp.int32)
    placed = (rolled + SHIFT) % total
    return ((placed + SHIFT) // WIN, total // WIN + 1, count)


def per_device(tokens, upstream, norm_gain, norm_bias, qkv_weight, qkv_bias, proj_weight):
    pieces = (tokens, upstream)
    pieces = move_third(move_second(move_first(pieces)))
    rolled, rolled_up = pieces
    depth_x, depth_y, depth_z, width = tokens.shape
    index_x, span_x, count_x = window_index(lax.axis_size("gx"), lax.axis_index("gx"), depth_x)
    index_y, span_y, count_y = window_index(lax.axis_size("gy"), lax.axis_index("gy"), depth_y)
    index_z, span_z, count_z = window_index(lax.axis_size("gz"), lax.axis_index("gz"), depth_z)
    idents = (index_x[:, None, None] * span_y + index_y[None, :, None]) * span_z + index_z[
        None, None, :
    ]
    token_wins = to_windows(rolled)
    up_wins = to_windows(rolled_up)
    ident_wins = to_windows(idents)
    zeros = (
        jnp.zeros((width, 3 * width), jnp.float32),
        jnp.zeros((3 * width,), jnp.float32),
        jnp.zeros((width, width), jnp.float32),
        jnp.zeros((width,), jnp.float32),
        jnp.zeros((width,), jnp.float32),
        jnp.zeros((width,), jnp.float32),
    )

    def advance(carry, item):
        grad_win, parts = window_grads(
            item[0], item[1], item[2], norm_gain, norm_bias, qkv_weight, qkv_bias, proj_weight
        )
        return (tuple((old + new for old, new in zip(carry, parts))), grad_win)

    totals, grad_wins = lax.scan(advance, zeros, (token_wins, up_wins, ident_wins))
    token_grad = from_windows(grad_wins, depth_x, depth_y, depth_z)
    summed = lax.psum(
        (totals[0], totals[1], totals[2], totals[3], totals[4], totals[5]), ("gx", "gy", "gz")
    )
    factor = float(depth_x * depth_y * depth_z * count_x * count_y * count_z) ** (-0.5)
    return (
        token_grad,
        summed[0] * factor,
        summed[1] * factor,
        summed[2] * factor,
        summed[3] * factor,
        summed[4] * factor,
        summed[5] * factor,
    )


def solution(mesh):
    placed = (P("gx", "gy", "gz", None), P("gx", "gy", "gz", None), P(), P(), P(), P(), P())
    return jax.shard_map(
        per_device,
        mesh=mesh,
        in_specs=placed,
        out_specs=(P("gx", "gy", "gz", None), P(), P(), P(), P(), P(), P()),
        check_vma=False,
    )
```

profile of v0, /device:TPU:6, one launch (start us, length us, event | category | flops | bytes accessed | tf_op | source)
XLA Modules:
  0.0 495.6 jit_solution(13295949907634760316)
XLA Ops:
  7.2 1.3 fusion.78
  9.4 1.3 fusion.77
  11.8 13.8 %collective-permute-done = bf16[4,16,16,192]{3,2,1,0:T(8,128)(2,1)S(1)} collective-permute-done((bf16[4,16,16,192]{3,2,1,0:T(8,128)(2,1)S(1)}, bf16[4,16,16,192]{3,2,1,0:T(8,128)(2,1)S(1)}, u32[]{:S(2)}, u32[]{:S(2)}) %collective-permute-start) | collective-permute-done | bytes 393248 | tf_op jit(solution)/shard_map/ppermute | solution.py:14
  25.7 9.9 %collective-permute-done.3 = bf16[4,16,16,192]{3,2,1,0:T(8,128)(2,1)S(1)} collective-permute-done((bf16[4,16,16,192]{3,2,1,0:T(8,128)(2,1)S(1)}, bf16[4,16,16,192]{3,2,1,0:T(8,128)(2,1)S(1)}, u32[]{:S(2)}, u32[]{:S(2)}) %collective-permute-start.3) | collective-permute-done | bytes 393248 | tf_op jit(solution)/shard_map/ppermute | solution.py:14
  36.1 9.7 %collective-permute-start.2 = (bf16[8,16,4,192]{3,2,1,0:T(4,128)(2,1)S(1)}, bf16[8,16,4,192]{3,2,1,0:T(4,128)(2,1)S(1)}, u32[]{:S(2)}, u32[]{:S(2)}) collective-permute-start(bf16[8,16,4,192]{3,2,1,0:T(4,128)(2,1)S(1)} %pad_maximum_fusion.7), channel_id=1, source_target_pairs={{0,7},{1,0},{2,1},{3,2},{4,3},{5,4},{6,5},{7,6},{8,15},{9,8},{10,9... | collective-permute-start | bytes 589832 | tf_op jit(solution)/shard_map/ppermute | solution.py:14
  46.6 1.1 collective-permute-start.5
  48.4 5.1 %collective-permute-done.2 = bf16[8,16,4,192]{3,2,1,0:T(4,128)(2,1)S(1)} collective-permute-done((bf16[8,16,4,192]{3,2,1,0:T(4,128)(2,1)S(1)}, bf16[8,16,4,192]{3,2,1,0:T(4,128)(2,1)S(1)}, u32[]{:S(2)}, u32[]{:S(2)}) %collective-permute-start.2) | collective-permute-done | bytes 196640 | tf_op jit(solution)/shard_map/ppermute | solution.py:14
  54.9 14.1 %collective-permute-done.5 = bf16[8,16,4,192]{3,2,1,0:T(4,128)(2,1)} collective-permute-done((bf16[8,16,4,192]{3,2,1,0:T(4,128)(2,1)}, bf16[8,16,4,192]{3,2,1,0:T(4,128)(2,1)}, u32[]{:S(2)}, u32[]{:S(2)}) %collective-permute-start.5) | collective-permute-done | bytes 196640 | tf_op jit(solution)/shard_map/ppermute | solution.py:14
  69.0 1.4 pad_maximum_fusion.4
  71.2 158.2 %while.23 = (s32[]{:T(128)}, f32[192,576]{1,0:T(8,128)S(1)}, f32[576]{0:T(1024)S(1)}, f32[192,192]{1,0:T(8,128)S(1)}, f32[192]{0:T(256)S(1)}, /*index=5*/f32[192...) while((s32[]{:T(128)}, f32[192,576]{1,0:T(8,128)S(1)}, ...), condition=%wide.region_12.13_spmd.clone, body=%wide.region_0.12_spmd.clone.sunk | while | flops 1065100416 | bytes 87224056 | solution.py:154
  71.9 1.4 fusion.144
  73.3 5.1 %fusion.146 = (f32[6,512]{1,0:T(8,128)S(1)}, f32[6,512,512]{1,2,0:T(8,128)}) fusion(pred[512,512]{0,1:T(8,128)(4,1)S(1)} %broadcast_compare_fusion.2, bf16[512,6,32]{0,2,1:T(8,128)(2,1)S(1)} %bitcast.162, bf16[512,6,32]{0,2,1:T(8,128)(2,1)S(1)} %bitcast.164), kind=kOutput, calls=%fused_computation.127.clone.1 | convolution fusion | flops 106955264 | bytes 6959104 | tf_op jit(solution)/shard_map/while/body/eval_jaxpr/sub | solution.py:39
  78.4 3.6 fusion.151
  83.0 1.0 fusion.147
  84.0 3.7 fusion.148
  87.7 10.8 %fusion.150 = bf16[6,32,512]{2,1,0:T(8,128)(2,1)S(1)} fusion(bf16[512,6,32]{0,2,1:T(8,128)(2,1)S(1)} %bitcast.165, f32[6,512,512]{1,2,0:T(8,128)} %fusion.148, f32[6,512,512]{1,2,0:T(8,128)} %get-tuple-element.353, f32[6,512]{1,0:T(8,128)S(1)} %get-tuple-element.354), kind=kOutput, calls=%fused_computation.22.clone.1 | convolution fusion | flops 111775232 | bytes 12988416 | tf_op jit(solution)/shard_map/while/body/eval_jaxpr/hqk,khd->qhd/dot_general | solution.py:53
  98.5 9.3 %fusion.149 = bf16[6,32,512]{2,1,0:T(8,128)(2,1)S(1)} fusion(bf16[512,6,32]{0,2,1:T(8,128)(2,1)S(1)} %bitcast.163, f32[6,512,512]{1,2,0:T(8,128)} %fusion.148, f32[6,512,512]{1,2,0:T(8,128)} %get-tuple-element.353, f32[6,512]{1,0:T(8,128)S(1)} %get-tuple-element.354), kind=kOutput, calls=%fused_computation.23.clone.1 | convolution fusion | flops 111775232 | bytes 12988416 | tf_op jit(solution)/shard_map/while/body/eval_jaxpr/hqk,qhd->khd/dot_general | solution.py:56
  108.0 1.4 fusion.152
  111.4 1.4 fusion.144
  112.8 5.1 %fusion.146 = (f32[6,512]{1,0:T(8,128)S(1)}, f32[6,512,512]{1,2,0:T(8,128)}) fusion(pred[512,512]{0,1:T(8,128)(4,1)S(1)} %broadcast_compare_fusion.2, bf16[512,6,32]{0,2,1:T(8,128)(2,1)S(1)} %bitcast.162, bf16[512,6,32]{0,2,1:T(8,128)(2,1)S(1)} %bitcast.164), kind=kOutput, calls=%fused_computation.127.clone.1 | convolution fusion | flops 106955264 | bytes 6959104 | tf_op jit(solution)/shard_map/while/body/eval_jaxpr/sub | solution.py:39
  117.9 3.6 fusion.151
  122.5 1.0 fusion.147
  123.6 3.7 fusion.148
  127.3 10.8 %fusion.150 = bf16[6,32,512]{2,1,0:T(8,128)(2,1)S(1)} fusion(bf16[512,6,32]{0,2,1:T(8,128)(2,1)S(1)} %bitcast.165, f32[6,512,512]{1,2,0:T(8,128)} %fusion.148, f32[6,512,512]{1,2,0:T(8,128)} %get-tuple-element.353, f32[6,512]{1,0:T(8,128)S(1)} %get-tuple-element.354), kind=kOutput, calls=%fused_computation.22.clone.1 | convolution fusion | flops 111775232 | bytes 12988416 | tf_op jit(solution)/shard_map/while/body/eval_jaxpr/hqk,khd->qhd/dot_general | solution.py:53
  138.1 9.3 %fusion.149 = bf16[6,32,512]{2,1,0:T(8,128)(2,1)S(1)} fusion(bf16[512,6,32]{0,2,1:T(8,128)(2,1)S(1)} %bitcast.163, f32[6,512,512]{1,2,0:T(8,128)} %fusion.148, f32[6,512,512]{1,2,0:T(8,128)} %get-tuple-element.353, f32[6,512]{1,0:T(8,128)S(1)} %get-tuple-element.354), kind=kOutput, calls=%fused_computation.23.clone.1 | convolution fusion | flops 111775232 | bytes 12988416 | tf_op jit(solution)/shard_map/while/body/eval_jaxpr/hqk,qhd->khd/dot_general | solution.py:56
  147.5 1.4 fusion.152
  150.9 1.4 fusion.144
  152.4 5.1 %fusion.146 = (f32[6,512]{1,0:T(8,128)S(1)}, f32[6,512,512]{1,2,0:T(8,128)}) fusion(pred[512,512]{0,1:T(8,128)(4,1)S(1)} %broadcast_compare_fusion.2, bf16[512,6,32]{0,2,1:T(8,128)(2,1)S(1)} %bitcast.162, bf16[512,6,32]{0,2,1:T(8,128)(2,1)S(1)} %bitcast.164), kind=kOutput, calls=%fused_computation.127.clone.1 | convolution fusion | flops 106955264 | bytes 6959104 | tf_op jit(solution)/shard_map/while/body/eval_jaxpr/sub | solution.py:39
  157.5 3.6 fusion.151
  162.1 1.0 fusion.147
  163.1 3.7 fusion.148
  166.8 10.8 %fusion.150 = bf16[6,32,512]{2,1,0:T(8,128)(2,1)S(1)} fusion(bf16[512,6,32]{0,2,1:T(8,128)(2,1)S(1)} %bitcast.165, f32[6,512,512]{1,2,0:T(8,128)} %fusion.148, f32[6,512,512]{1,2,0:T(8,128)} %get-tuple-element.353, f32[6,512]{1,0:T(8,128)S(1)} %get-tuple-element.354), kind=kOutput, calls=%fused_computation.22.clone.1 | convolution fusion | flops 111775232 | bytes 12988416 | tf_op jit(solution)/shard_map/while/body/eval_jaxpr/hqk,khd->qhd/dot_general | solution.py:53
  177.6 9.3 %fusion.149 = bf16[6,32,512]{2,1,0:T(8,128)(2,1)S(1)} fusion(bf16[512,6,32]{0,2,1:T(8,128)(2,1)S(1)} %bitcast.163, f32[6,512,512]{1,2,0:T(8,128)} %fusion.148, f32[6,512,512]{1,2,0:T(8,128)} %get-tuple-element.353, f32[6,512]{1,0:T(8,128)S(1)} %get-tuple-element.354), kind=kOutput, calls=%fused_computation.23.clone.1 | convolution fusion | flops 111775232 | bytes 12988416 | tf_op jit(solution)/shard_map/while/body/eval_jaxpr/hqk,qhd->khd/dot_general | solution.py:56
  187.1 1.4 fusion.152
  190.5 1.4 fusion.144
  191.9 5.1 %fusion.146 = (f32[6,512]{1,0:T(8,128)S(1)}, f32[6,512,512]{1,2,0:T(8,128)}) fusion(pred[512,512]{0,1:T(8,128)(4,1)S(1)} %broadcast_compare_fusion.2, bf16[512,6,32]{0,2,1:T(8,128)(2,1)S(1)} %bitcast.162, bf16[512,6,32]{0,2,1:T(8,128)(2,1)S(1)} %bitcast.164), kind=kOutput, calls=%fused_computation.127.clone.1 | convolution fusion | flops 106955264 | bytes 6959104 | tf_op jit(solution)/shard_map/while/body/eval_jaxpr/sub | solution.py:39
  197.0 3.6 fusion.151
  201.6 1.0 fusion.147
  202.7 3.7 fusion.148
  206.4 10.8 %fusion.150 = bf16[6,32,512]{2,1,0:T(8,128)(2,1)S(1)} fusion(bf16[512,6,32]{0,2,1:T(8,128)(2,1)S(1)} %bitcast.165, f32[6,512,512]{1,2,0:T(8,128)} %fusion.148, f32[6,512,512]{1,2,0:T(8,128)} %get-tuple-element.353, f32[6,512]{1,0:T(8,128)S(1)} %get-tuple-element.354), kind=kOutput, calls=%fused_computation.22.clone.1 | convolution fusion | flops 111775232 | bytes 12988416 | tf_op jit(solution)/shard_map/while/body/eval_jaxpr/hqk,khd->qhd/dot_general | solution.py:53
  217.2 9.3 %fusion.149 = bf16[6,32,512]{2,1,0:T(8,128)(2,1)S(1)} fusion(bf16[512,6,32]{0,2,1:T(8,128)(2,1)S(1)} %bitcast.163, f32[6,512,512]{1,2,0:T(8,128)} %fusion.148, f32[6,512,512]{1,2,0:T(8,128)} %get-tuple-element.353, f32[6,512]{1,0:T(8,128)S(1)} %get-tuple-element.354), kind=kOutput, calls=%fused_computation.23.clone.1 | convolution fusion | flops 111775232 | bytes 12988416 | tf_op jit(solution)/shard_map/while/body/eval_jaxpr/hqk,qhd->khd/dot_general | solution.py:56
  226.6 1.4 fusion.152
  230.3 76.7 %all-reduce = (f32[576]{0:T(1024)S(1)}, f32[192]{0:T(256)S(1)}, f32[192]{0:T(256)S(1)}, f32[192]{0:T(256)S(1)}) all-reduce(f32[576]{0:T(1024)S(1)} %get-tuple-element.97, f32[192]{0:T(256)S(1)} %get-tuple-element.99, f32[192]{0:T(256)S(1)} %get-tuple-element.100, ...), channel_id=1, replica_groups=mesh['gx'=16,'gy'=2,'gz'=8] {'gx','gy','gz'}, use_global_device_ids=true, to_apply=%region_14.15 | all-reduce | flops 1152 | bytes 9216 | tf_op jit(solution)/shard_map/psum | solution.py:156
  308.1 1.4 copy.38
  309.6 1.1 copy.39
  311.2 174.0 %all-reduce.4.cloned.1.call-done = (f32[192,576]{1,0:T(8,128)}, f32[192,192]{1,0:T(8,128)}) async-done(((f32[192,576]{1,0:T(8,128)}, f32[192,192]{1,0:T(8,128)}), (f32[192,576]{1,0:T(8,128)}, f32[192,192]{1,0:T(8,128)})) %all-reduce.4.cloned.1.call-update) | async-done | bytes 589840 | tf_op jit(solution)/shard_map/psum | solution.py:156
  485.2 1.9 broadcast_multiply_fusion.3
  487.1 1.6 broadcast_multiply_fusion.4
  (131 shorter events, 21.1 us)
Async XLA Ops:
  7.2 478.1 %all-reduce.4.cloned.1.call-start = ((), (), s32[]{:S(2)}) async-start(), calls=%async_computation | async-start | bytes 1376256 | tf_op jit(solution)/shard_map/psum | solution.py:156
  8.5 17.0 %collective-permute-start = (bf16[4,16,16,192]{3,2,1,0:T(8,128)(2,1)S(1)}, bf16[4,16,16,192]{3,2,1,0:T(8,128)(2,1)S(1)}, u32[]{:S(2)}, u32[]{:S(2)}) collective-permute-start(bf16[4,16,16,192]{3,2,1,0:T(8,128)(2,1)S(1)} %get-tuple-element.238), channel_id=1, source_target_pairs={{0,240},{16,0},{32,16},{48,32},{64,48},{80,64},{96,80},{112,96},{1... | collective-permute-start | bytes 1179656 | tf_op jit(solution)/shard_map/ppermute | solution.py:14
  10.7 24.9 %collective-permute-start.3 = (bf16[4,16,16,192]{3,2,1,0:T(8,128)(2,1)S(1)}, bf16[4,16,16,192]{3,2,1,0:T(8,128)(2,1)S(1)}, u32[]{:S(2)}, u32[]{:S(2)}) collective-permute-start(bf16[4,16,16,192]{3,2,1,0:T(8,128)(2,1)S(1)} %get-tuple-element.236), channel_id=1, source_target_pairs={{0,240},{16,0},{32,16},{48,32},{64,48},{80,64},{96,80},{112,96},{1... | collective-permute-start | bytes 1179656 | tf_op jit(solution)/shard_map/ppermute | solution.py:14
  25.6 10.5 %collective-permute-start.1 = (bf16[8,4,16,192]{3,2,1,0:T(8,128)(2,1)S(1)}, bf16[8,4,16,192]{3,2,1,0:T(8,128)(2,1)S(1)}, u32[]{:S(2)}, u32[]{:S(2)}) collective-permute-start(bf16[8,4,16,192]{3,2,1,0:T(8,128)(2,1)S(1)} %pad_maximum_fusion.8), channel_id=1, source_target_pairs={{0,8},{8,0},{1,9},{9,1},{2,10},{10,2},{3,11},{11,3},{4,12},{12,4},... | collective-permute-start | bytes 589832 | tf_op jit(solution)/shard_map/ppermute | solution.py:14
  35.7 10.2 %collective-permute-start.4 = (bf16[8,4,16,192]{3,2,1,0:T(8,128)(2,1)S(1)}, bf16[8,4,16,192]{3,2,1,0:T(8,128)(2,1)S(1)}, u32[]{:S(2)}, u32[]{:S(2)}) collective-permute-start(bf16[8,4,16,192]{3,2,1,0:T(8,128)(2,1)S(1)} %pad_maximum_fusion.6), channel_id=1, source_target_pairs={{0,8},{8,0},{1,9},{9,1},{2,10},{10,2},{3,11},{11,3},{4,12},{12,4},... | collective-permute-start | bytes 589832 | tf_op jit(solution)/shard_map/ppermute | solution.py:14
  36.1 17.4 %collective-permute-start.2 = (bf16[8,16,4,192]{3,2,1,0:T(4,128)(2,1)S(1)}, bf16[8,16,4,192]{3,2,1,0:T(4,128)(2,1)S(1)}, u32[]{:S(2)}, u32[]{:S(2)}) collective-permute-start(bf16[8,16,4,192]{3,2,1,0:T(4,128)(2,1)S(1)} %pad_maximum_fusion.7), channel_id=1, source_target_pairs={{0,7},{1,0},{2,1},{3,2},{4,3},{5,4},{6,5},{7,6},{8,15},{9,8},{10,9... | collective-permute-start | bytes 589832 | tf_op jit(solution)/shard_map/ppermute | solution.py:14
  46.6 22.4 %collective-permute-start.5 = (bf16[8,16,4,192]{3,2,1,0:T(4,128)(2,1)}, bf16[8,16,4,192]{3,2,1,0:T(4,128)(2,1)}, u32[]{:S(2)}, u32[]{:S(2)}) collective-permute-start(bf16[8,16,4,192]{3,2,1,0:T(4,128)(2,1)} %pad_maximum_fusion.5), channel_id=1, source_target_pairs={{0,7},{1,0},{2,1},{3,2},{4,3},{5,4},{6,5},{7,6},{8,15},{9,8},{10,9... | collective-permute-start | bytes 589832 | tf_op jit(solution)/shard_map/ppermute | solution.py:14
  48.3 22.8 %copy-start.1 = (bf16[192,192]{1,0:T(8,128)(2,1)S(1)}, bf16[192,192]{1,0:T(8,128)(2,1)}, u32[]{:S(2)}) copy-start(bf16[192,192]{1,0:T(8,128)(2,1)} %param.15) | copy-start | bytes 221188
  48.3 22.8 %copy-start.4 = (f32[192]{0:T(256)S(1)}, f32[192]{0:T(256)}, u32[]{:S(2)}) copy-start(f32[192]{0:T(256)} %param.11) | copy-start | bytes 2308
  48.4 22.8 %copy-start.5 = (f32[576]{0:T(1024)S(1)}, f32[576]{0:T(1024)}, u32[]{:S(2)}) copy-start(f32[576]{0:T(1024)} %param.14) | copy-start | bytes 6916
  48.4 22.8 %copy-start.6 = (f32[192]{0:T(256)S(1)}, f32[192]{0:T(256)}, u32[]{:S(2)}) copy-start(f32[192]{0:T(256)} %param.12) | copy-start | bytes 2308
  54.9 16.3 %copy-start.2 = (f32[192,576]{1,0:T(8,128)S(1)}, f32[192,576]{1,0:T(8,128)}, u32[]{:S(2)}) copy-start(f32[192,576]{1,0:T(8,128)} %custom-call) | copy-start | bytes 1327108
  78.4 4.6 copy-start.7
  117.9 4.6 copy-start.7
  157.5 4.6 copy-start.7
  197.0 4.6 copy-start.7
  229.4 0.7 copy-start
  229.4 0.8 copy-start.3
Sparse Core Ops, SparseCore 0:
  230.4 254.8 all-reduce.3
where the time goes:
time: 496 us
  waiting for transfers between devices  217 us (44%)
  matrix products  149 us (30%)
  blocking collectives  76.7 us (15%)
  other arithmetic  15.2 us (3%)
  between operations  14.3 us (3%)
  starting transfers between devices  12.5 us (3%)
  local copies, waits for them, and re-layouts  10.6 us (2%)
    psum x1, waiting for transfers between devices, per_device(): lax.psum((totals[0], totals[1], totals[2], totals[3], totals[4], totals[5...  174 us
    psum x1, blocking collectives, per_device(): lax.psum((totals[0], totals[1], totals[2], totals[3], totals[4], totals[5...  76.7 us
    dot_general x4, matrix products, window_grads(): jnp.einsum('hqk,khd->qhd', score_grad, keyset, preferred_element_type=sin...  43.1 us
    ppermute x6, waiting for transfers between devices, passed_along(): return lax.ppermute(value, axis, pairs)  42.9 us
    dot_general x4, matrix products, window_grads(): jnp.einsum('hqk,qhd->khd', score_grad, query, preferred_element_type=single)  37 us
    sub x4, matrix products, window_grads(): expo = jnp.exp(scores - peak)  20.4 us
    dot_general x4, matrix products, window_grads(): jnp.einsum('qhd,khd->hqk', attended_grad, valset, preferred_element_type=...  14.8 us
    dot_general x4, matrix products, window_grads(): jnp.einsum('hqk,khd->qhd', probs_half, valset, preferred_element_type=sin...  14.3 us
  transfers between devices with their start and end apart: 7, of which 5 were waited for; matrix products, arithmetic and copies ran while one was open for 2% of the time, Pallas kernels for 0%

commit v1 on v0

--- a/solution.py
+++ b/solution.py
@@ -154,7 +154,8 @@
     totals, grad_wins = lax.scan(advance, zeros, (token_wins, up_wins, ident_wins))
     token_grad = from_windows(grad_wins, depth_x, depth_y, depth_z)
     summed = lax.psum(
-        (totals[0], totals[1], totals[2], totals[3], totals[4], totals[5]), ("gx", "gy", "gz")
+        lax.psum((totals[0], totals[1], totals[2], totals[3], totals[4], totals[5]), ("gy", "gz")),
+        "gx",
     )
     factor = float(depth_x * depth_y * depth_z * count_x * count_y * count_z) ** (-0.5)
     return (

time: 496 us -> 599 us (1.21)
  waiting for transfers between devices: 217 us -> 302 us
  blocking collectives: 76.7 us -> 83.5 us
  matrix products: 149 us -> 155 us
    psum x0 -> x1, waiting for transfers between devices: none -> 157 us  [per_device(): lax.psum(lax.psum((totals[0], totals[1], totals[2], totals[3], totals[4],...]
    psum x1, waiting for transfers between devices: 174 us -> 101 us  [per_device(): lax.psum((totals[0], totals[1], totals[2], totals[3], totals[4], totals[5...]
    psum x0 -> x1, blocking collectives: none -> 31.7 us  [per_device(): lax.psum(lax.psum((totals[0], totals[1], totals[2], totals[3], totals[4],...]
    psum x1, blocking collectives: 76.7 us -> 51.8 us  [per_device(): lax.psum((totals[0], totals[1], totals[2], totals[3], totals[4], totals[5...]
    dot_general x4, matrix products: 1.69 us -> 7.82 us  [window_grads(): jnp.einsum('lc,lf->cf', hidden, packed_grad, preferred_element_type=single)]
  transfers between devices with their start and end apart: 7 -> 8, of which waited for: 5 -> 6; matrix products, arithmetic and copies ran while one was open for 2% -> 2% of each run, Pallas kernels for 0% -> 0%
where the time goes in v1:
time: 599 us; the launch traced here: 594 us
  waiting for transfers between devices  302 us (50%)
  matrix products  155 us (26%)
  blocking collectives  83.5 us (14%)
  other arithmetic  15.1 us (3%)
  between operations  14.3 us (2%)
  starting transfers between devices  12.5 us (2%)
  local copies, waits for them, and re-layouts  11.3 us (2%)
    psum x1, waiting for transfers between devices, per_device(): lax.psum(lax.psum((totals[0], totals[1], totals[2], totals[3], totals[4],...  157 us
    psum x1, waiting for transfers between devices, per_device(): lax.psum((totals[0], totals[1], totals[2], totals[3], totals[4], totals[5...  101 us
    psum x1, blocking collectives, per_device(): lax.psum((totals[0], totals[1], totals[2], totals[3], totals[4], totals[5...  51.8 us
    ppermute x6, waiting for transfers between devices, passed_along(): return lax.ppermute(value, axis, pairs)  43.2 us
    dot_general x4, matrix products, window_grads(): jnp.einsum('hqk,khd->qhd', score_grad, keyset, preferred_element_type=sin...  43.1 us
    dot_general x4, matrix products, window_grads(): jnp.einsum('hqk,qhd->khd', score_grad, query, preferred_element_type=single)  37.1 us
    psum x1, blocking collectives, per_device(): lax.psum(lax.psum((totals[0], totals[1], totals[2], totals[3], totals[4],...  31.7 us
    sub x4, matrix products, window_grads(): expo = jnp.exp(scores - peak)  20.4 us
  transfers between devices with their start and end apart: 8, of which 6 were waited for; matrix products, arithmetic and copies ran while one was open for 2% of the time, Pallas kernels for 0%

profile of v1, /device:TPU:6, one launch (start us, length us, event | category | flops | bytes accessed | tf_op | source)
XLA Modules:
  0.0 593.5 jit_solution(16049172843050234554)
XLA Ops:
  7.2 2.1 fusion.78
  10.1 1.3 fusion.77
  12.5 14.0 %collective-permute-done = bf16[4,16,16,192]{3,2,1,0:T(8,128)(2,1)S(1)} collective-permute-done((bf16[4,16,16,192]{3,2,1,0:T(8,128)(2,1)}, bf16[4,16,16,192]{3,2,1,0:T(8,128)(2,1)S(1)}, u32[]{:S(2)}, u32[]{:S(2)}) %collective-permute-start) | collective-permute-done | bytes 393248 | tf_op jit(solution)/shard_map/ppermute | solution.py:14
  26.6 9.9 %collective-permute-done.3 = bf16[4,16,16,192]{3,2,1,0:T(8,128)(2,1)S(1)} collective-permute-done((bf16[4,16,16,192]{3,2,1,0:T(8,128)(2,1)S(1)}, bf16[4,16,16,192]{3,2,1,0:T(8,128)(2,1)S(1)}, u32[]{:S(2)}, u32[]{:S(2)}) %collective-permute-start.3) | collective-permute-done | bytes 393248 | tf_op jit(solution)/shard_map/ppermute | solution.py:14
  37.1 9.7 %collective-permute-start.2 = (bf16[8,16,4,192]{3,2,1,0:T(4,128)(2,1)S(1)}, bf16[8,16,4,192]{3,2,1,0:T(4,128)(2,1)S(1)}, u32[]{:S(2)}, u32[]{:S(2)}) collective-permute-start(bf16[8,16,4,192]{3,2,1,0:T(4,128)(2,1)S(1)} %pad_maximum_fusion.7), channel_id=1, source_target_pairs={{0,7},{1,0},{2,1},{3,2},{4,3},{5,4},{6,5},{7,6},{8,15},{9,8},{10,9... | collective-permute-start | bytes 589832 | tf_op jit(solution)/shard_map/ppermute | solution.py:14
  49.3 5.1 collective-permute-done.2
  55.8 14.1 %collective-permute-done.5 = bf16[8,16,4,192]{3,2,1,0:T(4,128)(2,1)} collective-permute-done((bf16[8,16,4,192]{3,2,1,0:T(4,128)(2,1)}, bf16[8,16,4,192]{3,2,1,0:T(4,128)(2,1)}, u32[]{:S(2)}, u32[]{:S(2)}) %collective-permute-start.5) | collective-permute-done | bytes 196640 | tf_op jit(solution)/shard_map/ppermute | solution.py:14
  69.9 1.4 pad_maximum_fusion.4
  72.1 164.3 %while.23 = (s32[]{:T(128)}, f32[192,576]{1,0:T(8,128)}, f32[576]{0:T(1024)S(1)}, f32[192,192]{1,0:T(8,128)S(1)}, f32[192]{0:T(256)S(1)}, /*index=5*/f32[192]{0:...) while((s32[]{:T(128)}, f32[192,576]{1,0:T(8,128)}, ...), condition=%wide.region_12.13_spmd.clone, body=%wide.region_0.12_spmd.clone.sunk | while | flops 1065100416 | bytes 87174904 | solution.py:154
  72.8 1.4 fusion.144
  74.2 5.1 fusion.146
  79.3 3.6 fusion.151
  84.9 3.7 fusion.148
  88.6 10.8 %fusion.150 = bf16[6,32,512]{2,1,0:T(8,128)(2,1)S(1)} fusion(bf16[512,6,32]{0,2,1:T(8,128)(2,1)S(1)} %bitcast.165, f32[6,512,512]{1,2,0:T(8,128)} %fusion.148, f32[6,512,512]{1,2,0:T(8,128)} %get-tuple-element.359, f32[6,512]{1,0:T(8,128)S(1)} %get-tuple-element.360), kind=kOutput, calls=%fused_computation.22.clone.1 | convolution fusion | flops 111775232 | bytes 12988416 | tf_op jit(solution)/shard_map/while/body/eval_jaxpr/hqk,khd->qhd/dot_general | solution.py:53
  99.4 9.3 %fusion.149 = bf16[6,32,512]{2,1,0:T(8,128)(2,1)S(1)} fusion(bf16[512,6,32]{0,2,1:T(8,128)(2,1)S(1)} %bitcast.163, f32[6,512,512]{1,2,0:T(8,128)} %fusion.148, f32[6,512,512]{1,2,0:T(8,128)} %get-tuple-element.359, f32[6,512]{1,0:T(8,128)S(1)} %get-tuple-element.360), kind=kOutput, calls=%fused_computation.23.clone.1 | convolution fusion | flops 111775232 | bytes 12988416 | tf_op jit(solution)/shard_map/while/body/eval_jaxpr/hqk,qhd->khd/dot_general | solution.py:56
  108.9 1.4 fusion.152
  110.3 1.2 convolution_add_fusion.5
  113.0 1.4 fusion.144
  114.5 5.1 fusion.146
  119.6 3.6 fusion.151
  125.2 3.7 fusion.148
  128.9 10.8 %fusion.150 = bf16[6,32,512]{2,1,0:T(8,128)(2,1)S(1)} fusion(bf16[512,6,32]{0,2,1:T(8,128)(2,1)S(1)} %bitcast.165, f32[6,512,512]{1,2,0:T(8,128)} %fusion.148, f32[6,512,512]{1,2,0:T(8,128)} %get-tuple-element.359, f32[6,512]{1,0:T(8,128)S(1)} %get-tuple-element.360), kind=kOutput, calls=%fused_computation.22.clone.1 | convolution fusion | flops 111775232 | bytes 12988416 | tf_op jit(solution)/shard_map/while/body/eval_jaxpr/hqk,khd->qhd/dot_general | solution.py:53
  139.7 9.3 %fusion.149 = bf16[6,32,512]{2,1,0:T(8,128)(2,1)S(1)} fusion(bf16[512,6,32]{0,2,1:T(8,128)(2,1)S(1)} %bitcast.163, f32[6,512,512]{1,2,0:T(8,128)} %fusion.148, f32[6,512,512]{1,2,0:T(8,128)} %get-tuple-element.359, f32[6,512]{1,0:T(8,128)S(1)} %get-tuple-element.360), kind=kOutput, calls=%fused_computation.23.clone.1 | convolution fusion | flops 111775232 | bytes 12988416 | tf_op jit(solution)/shard_map/while/body/eval_jaxpr/hqk,qhd->khd/dot_general | solution.py:56
  149.2 1.4 fusion.152
  150.6 2.2 convolution_add_fusion.5
  154.4 1.4 fusion.144
  155.8 5.1 fusion.146
  160.9 3.6 fusion.151
  166.6 3.7 fusion.148
  170.3 10.8 %fusion.150 = bf16[6,32,512]{2,1,0:T(8,128)(2,1)S(1)} fusion(bf16[512,6,32]{0,2,1:T(8,128)(2,1)S(1)} %bitcast.165, f32[6,512,512]{1,2,0:T(8,128)} %fusion.148, f32[6,512,512]{1,2,0:T(8,128)} %get-tuple-element.359, f32[6,512]{1,0:T(8,128)S(1)} %get-tuple-element.360), kind=kOutput, calls=%fused_computation.22.clone.1 | convolution fusion | flops 111775232 | bytes 12988416 | tf_op jit(solution)/shard_map/while/body/eval_jaxpr/hqk,khd->qhd/dot_general | solution.py:53
  181.1 9.3 %fusion.149 = bf16[6,32,512]{2,1,0:T(8,128)(2,1)S(1)} fusion(bf16[512,6,32]{0,2,1:T(8,128)(2,1)S(1)} %bitcast.163, f32[6,512,512]{1,2,0:T(8,128)} %fusion.148, f32[6,512,512]{1,2,0:T(8,128)} %get-tuple-element.359, f32[6,512]{1,0:T(8,128)S(1)} %get-tuple-element.360), kind=kOutput, calls=%fused_computation.23.clone.1 | convolution fusion | flops 111775232 | bytes 12988416 | tf_op jit(solution)/shard_map/while/body/eval_jaxpr/hqk,qhd->khd/dot_general | solution.py:56
  190.5 1.4 fusion.152
  192.0 2.2 convolution_add_fusion.5
  195.7 1.4 fusion.144
  197.1 5.1 fusion.146
  202.2 3.6 fusion.151
  207.9 3.7 fusion.148
  211.6 10.8 %fusion.150 = bf16[6,32,512]{2,1,0:T(8,128)(2,1)S(1)} fusion(bf16[512,6,32]{0,2,1:T(8,128)(2,1)S(1)} %bitcast.165, f32[6,512,512]{1,2,0:T(8,128)} %fusion.148, f32[6,512,512]{1,2,0:T(8,128)} %get-tuple-element.359, f32[6,512]{1,0:T(8,128)S(1)} %get-tuple-element.360), kind=kOutput, calls=%fused_computation.22.clone.1 | convolution fusion | flops 111775232 | bytes 12988416 | tf_op jit(solution)/shard_map/while/body/eval_jaxpr/hqk,khd->qhd/dot_general | solution.py:53
  222.4 9.3 %fusion.149 = bf16[6,32,512]{2,1,0:T(8,128)(2,1)S(1)} fusion(bf16[512,6,32]{0,2,1:T(8,128)(2,1)S(1)} %bitcast.163, f32[6,512,512]{1,2,0:T(8,128)} %fusion.148, f32[6,512,512]{1,2,0:T(8,128)} %get-tuple-element.359, f32[6,512]{1,0:T(8,128)S(1)} %get-tuple-element.360), kind=kOutput, calls=%fused_computation.23.clone.1 | convolution fusion | flops 111775232 | bytes 12988416 | tf_op jit(solution)/shard_map/while/body/eval_jaxpr/hqk,qhd->khd/dot_general | solution.py:56
  231.8 1.4 fusion.152
  233.3 2.2 convolution_add_fusion.5
  237.1 1.4 copy.38
  239.6 51.8 %all-reduce = (f32[576]{0:T(1024)S(1)}, f32[192]{0:T(256)S(1)}, f32[192]{0:T(256)S(1)}, f32[192]{0:T(256)S(1)}) all-reduce(f32[576]{0:T(1024)S(1)} %get-tuple-element.97, f32[192]{0:T(256)S(1)} %get-tuple-element.99, f32[192]{0:T(256)S(1)} %get-tuple-element.100, ...), channel_id=1, replica_groups=mesh['gx'=16,'gy'=2,'gz'=8] {'gy','gz'}, use_global_device_ids=true, to_apply=%region_15.16 | all-reduce | flops 1152 | bytes 9216 | tf_op jit(solution)/shard_map/psum | solution.py:157
  291.4 31.7 %all-reduce.2 = (f32[576]{0:T(1024)S(1)}, f32[192]{0:T(256)S(1)}, f32[192]{0:T(256)S(1)}, f32[192]{0:T(256)S(1)}) all-reduce(f32[576]{0:T(1024)S(1)} %get-tuple-element.221, f32[192]{0:T(256)S(1)} %get-tuple-element.222, f32[192]{0:T(256)S(1)} %get-tuple-element.223, ...), channel_id=1, replica_groups=mesh['gx'=16,'gy'=2,'gz'=8] {'gx'}, use_global_device_ids=true, to_apply=%region_16.17 | all-reduce | flops 1152 | bytes 9216 | tf_op jit(solution)/shard_map/psum | solution.py:156
  323.2 100.8 %all-reduce.7.cloned.1.call-done = (f32[192,576]{1,0:T(8,128)}, f32[192,192]{1,0:T(8,128)}) async-done(((f32[192,576]{1,0:T(8,128)}, f32[192,192]{1,0:T(8,128)}), (f32[192,576]{1,0:T(8,128)}, f32[192,192]{1,0:T(8,128)})) %all-reduce.7.cloned.1.call-update) | async-done | bytes 589840 | tf_op jit(solution)/shard_map/psum | solution.py:157
  425.7 157.5 %all-reduce.9.cloned.1.call-done = (f32[192,576]{1,0:T(8,128)}, f32[192,192]{1,0:T(8,128)}) async-done(((f32[192,576]{1,0:T(8,128)}, f32[192,192]{1,0:T(8,128)}), (f32[192,576]{1,0:T(8,128)}, f32[192,192]{1,0:T(8,128)})) %all-reduce.9.cloned.1.call-update) | async-done | bytes 589840 | tf_op jit(solution)/shard_map/psum | solution.py:156
  583.2 1.9 broadcast_multiply_fusion.3
  585.1 1.6 broadcast_multiply_fusion.4
  (131 shorter events, 25.5 us)
Async XLA Ops:
  7.2 416.8 %all-reduce.7.cloned.1.call-start = ((), (), s32[]{:S(2)}) async-start(), calls=%async_computation | async-start | bytes 1376256 | tf_op jit(solution)/shard_map/psum | solution.py:157
  9.3 17.1 %collective-permute-start = (bf16[4,16,16,192]{3,2,1,0:T(8,128)(2,1)}, bf16[4,16,16,192]{3,2,1,0:T(8,128)(2,1)S(1)}, u32[]{:S(2)}, u32[]{:S(2)}) collective-permute-start(bf16[4,16,16,192]{3,2,1,0:T(8,128)(2,1)} %get-tuple-element.244), channel_id=1, source_target_pairs={{0,240},{16,0},{32,16},{48,32},{64,48},{80,64},{96,80},{112,96},{1... | collective-permute-start | bytes 1179656 | tf_op jit(solution)/shard_map/ppermute | solution.py:14
  11.4 25.1 %collective-permute-start.3 = (bf16[4,16,16,192]{3,2,1,0:T(8,128)(2,1)S(1)}, bf16[4,16,16,192]{3,2,1,0:T(8,128)(2,1)S(1)}, u32[]{:S(2)}, u32[]{:S(2)}) collective-permute-start(bf16[4,16,16,192]{3,2,1,0:T(8,128)(2,1)S(1)} %get-tuple-element.242), channel_id=1, source_target_pairs={{0,240},{16,0},{32,16},{48,32},{64,48},{80,64},{96,80},{112,96},{1... | collective-permute-start | bytes 1179656 | tf_op jit(solution)/shard_map/ppermute | solution.py:14
  26.5 10.5 %collective-permute-start.1 = (bf16[8,4,16,192]{3,2,1,0:T(8,128)(2,1)S(1)}, bf16[8,4,16,192]{3,2,1,0:T(8,128)(2,1)S(1)}, u32[]{:S(2)}, u32[]{:S(2)}) collective-permute-start(bf16[8,4,16,192]{3,2,1,0:T(8,128)(2,1)S(1)} %pad_maximum_fusion.8), channel_id=1, source_target_pairs={{0,8},{8,0},{1,9},{9,1},{2,10},{10,2},{3,11},{11,3},{4,12},{12,4},... | collective-permute-start | bytes 589832 | tf_op jit(solution)/shard_map/ppermute | solution.py:14
  36.6 10.2 %collective-permute-start.4 = (bf16[8,4,16,192]{3,2,1,0:T(8,128)(2,1)S(1)}, bf16[8,4,16,192]{3,2,1,0:T(8,128)(2,1)S(1)}, u32[]{:S(2)}, u32[]{:S(2)}) collective-permute-start(bf16[8,4,16,192]{3,2,1,0:T(8,128)(2,1)S(1)} %pad_maximum_fusion.6), channel_id=1, source_target_pairs={{0,8},{8,0},{1,9},{9,1},{2,10},{10,2},{3,11},{11,3},{4,12},{12,4},... | collective-permute-start | bytes 589832 | tf_op jit(solution)/shard_map/ppermute | solution.py:14
  37.1 17.4 %collective-permute-start.2 = (bf16[8,16,4,192]{3,2,1,0:T(4,128)(2,1)S(1)}, bf16[8,16,4,192]{3,2,1,0:T(4,128)(2,1)S(1)}, u32[]{:S(2)}, u32[]{:S(2)}) collective-permute-start(bf16[8,16,4,192]{3,2,1,0:T(4,128)(2,1)S(1)} %pad_maximum_fusion.7), channel_id=1, source_target_pairs={{0,7},{1,0},{2,1},{3,2},{4,3},{5,4},{6,5},{7,6},{8,15},{9,8},{10,9... | collective-permute-start | bytes 589832 | tf_op jit(solution)/shard_map/ppermute | solution.py:14
  47.6 22.4 %collective-permute-start.5 = (bf16[8,16,4,192]{3,2,1,0:T(4,128)(2,1)}, bf16[8,16,4,192]{3,2,1,0:T(4,128)(2,1)}, u32[]{:S(2)}, u32[]{:S(2)}) collective-permute-start(bf16[8,16,4,192]{3,2,1,0:T(4,128)(2,1)} %pad_maximum_fusion.5), channel_id=1, source_target_pairs={{0,7},{1,0},{2,1},{3,2},{4,3},{5,4},{6,5},{7,6},{8,15},{9,8},{10,9... | collective-permute-start | bytes 589832 | tf_op jit(solution)/shard_map/ppermute | solution.py:14
  49.2 22.8 %copy-start.1 = (bf16[192,192]{1,0:T(8,128)(2,1)S(1)}, bf16[192,192]{1,0:T(8,128)(2,1)}, u32[]{:S(2)}) copy-start(bf16[192,192]{1,0:T(8,128)(2,1)} %param.15) | copy-start | bytes 221188
  49.3 22.8 %copy-start.2 = (f32[192]{0:T(256)S(1)}, f32[192]{0:T(256)}, u32[]{:S(2)}) copy-start(f32[192]{0:T(256)} %param.11) | copy-start | bytes 2308
  49.3 22.8 %copy-start.3 = (f32[576]{0:T(1024)S(1)}, f32[576]{0:T(1024)}, u32[]{:S(2)}) copy-start(f32[576]{0:T(1024)} %param.14) | copy-start | bytes 6916
  49.3 22.8 %copy-start.4 = (f32[192]{0:T(256)S(1)}, f32[192]{0:T(256)}, u32[]{:S(2)}) copy-start(f32[192]{0:T(256)} %param.12) | copy-start | bytes 2308
  79.3 4.6 copy-start.5
  119.6 4.6 copy-start.5
  160.9 4.6 copy-start.5
  202.2 4.6 copy-start.5
  236.4 0.7 copy-start
  237.1 346.1 %all-reduce.9.cloned.1.call-start = ((), (), s32[]{:S(2)}) async-start(), calls=%async_computation.1 | async-start | bytes 1376256 | tf_op jit(solution)/shard_map/psum | solution.py:156
Sparse Core Ops, SparseCore 0:
  237.2 186.7 all-reduce.6
  426.9 156.2 all-reduce.8
